TPU v7x, 32 devices: a whole 2x2x4 slice. The times are simulated.
32 devices in a mesh: parts: 2 (over y), step: 4 (over z), frame: 2 (over x), head: 2 (over core).
Axes of the slice: x: 2, y: 2, z: 4, core: 2. Of those that a mesh axis runs over, the one named last changes fastest.
Arguments:
- start_noise: float32 [32, 256], P('parts', 'frame'), parts along dimension 0, may hold values from -6 to 6
- position: bfloat16 [256, 1152], P('frame'), may hold values from -6 to 6
- time_table: bfloat16 [128, 1152], replicated, may hold values from -6 to 6
- time_index: int32 [4], P('step'), may hold values from 0 to 127
- sched_index: int32 [4], P('step'), may hold values from 0 to 127
- coef_keep: float32 [128], replicated, may hold values from -0.06 to -0.01
- coef_noise: float32 [128], replicated, may hold values from 0.03 to 0.12
- w_in: bfloat16 [16, 1152], replicated, may hold values from -1.5 to 1.5
- norm_gain: float32 [1152], replicated, may hold values from 0.5 to 1.5
- w_qkv: bfloat16 [1152, 3, 1152], P('step', None, 'head'), may hold values from -4 to 4
- w_proj: bfloat16 [1152, 1152], P('step', 'head'), may hold values from -0.1875 to 0.1875
- w_final: bfloat16 [16, 1152], replicated, may hold values from -0.1875 to 0.1875
Outputs:
- trajectory: float32 [4, 32, 256], P('step', 'parts', 'frame'), parts along dimension 1
- residual_norms: float32 [8], P('parts'), parts along dimension 0
There are 2 independent parts, one for each index of `parts`. A program takes and returns all parts, laid end to end along the dimension named above; an argument that names none is the same for every part. Nothing has to cross between parts.
All inputs are finite; a program needn't handle non-finite values.
Results may differ from a plain program's by a relative error of at most 0.0044.
Values may be sent and summed in bfloat16 or wider, within the bound.
A program may use at most 64 MiB of HBM per device.

v0:
```python
import math
import jax
import jax.numpy as jnp
from jax import lax
from jax.sharding import PartitionSpec as P

HDIM = 72
ITERS = 4


def entering(value, axis, combine, identity):
    count, here = (lax.axis_size(axis), lax.axis_index(axis))
    everything = lax.all_gather(value, axis)
    start = jnp.broadcast_to(jnp.asarray(identity, value.dtype), value.shape)

    def hop(k, before):
        reached = k < here
        new = combine(before, everything[k])
        return jnp.where(reached, new, before)

    return lax.fori_loop(0, count, hop, start)


def add_terms(first, second):
    return first + second


def local(
    start_noise,
    position,
    time_table,
    time_index,
    sched_index,
    coef_keep,
    coef_noise,
    w_in,
    norm_gain,
    w_qkv,
    w_proj,
    w_final,
):
    w_qkv_all, w_proj_all = (
        lax.all_gather(w_qkv, "step", axis=0, tiled=True),
        lax.all_gather(w_proj, "step", axis=0, tiled=True),
    )
    batch_steps = time_index.shape[0]
    row_count = start_noise.shape[1]
    table_rows = time_table.shape[0]
    pick_time = (time_index[:, None] == jnp.arange(table_rows)[None, :]).astype(jnp.bfloat16)
    time_embed = jnp.dot(pick_time, time_table, preferred_element_type=jnp.float32)
    pick_sched = (sched_index[:, None] == jnp.arange(table_rows)[None, :]).astype(jnp.float32)
    keep_rate = jnp.sum(pick_sched * coef_keep[None, :], axis=1)
    noise_rate = jnp.sum(pick_sched * coef_noise[None, :], axis=1)
    heads_local = w_qkv_all.shape[2] // HDIM
    cell_count = (
        batch_steps
        * lax.axis_size("step")
        * start_noise.shape[0]
        * row_count
        * lax.axis_size("frame")
    )
    states = start_noise[None]
    drift_term = jnp.zeros_like(states)
    residual_list = []
    for iteration in range(ITERS):
        latent_bf = states.astype(jnp.bfloat16)
        hidden = (
            jnp.einsum("bcr,cd->brd", latent_bf, w_in, preferred_element_type=jnp.float32)
            + position
            + time_embed[:, None, :]
        )
        normed = (
            hidden * lax.rsqrt(jnp.mean(hidden * hidden, axis=2, keepdims=True) + 1e-06) * norm_gain
        ).astype(jnp.bfloat16)
        projected = jnp.einsum(
            "brd,dkq->brkq", normed, w_qkv_all, preferred_element_type=jnp.float32
        ).astype(jnp.bfloat16)
        queries = projected[:, :, 0].reshape(batch_steps, row_count, heads_local, HDIM)
        score_scale = 1.0 / math.sqrt(HDIM)
        keys_values = projected[:, :, 1:3]
        piece = lax.all_gather(keys_values, "frame", axis=1, tiled=True)
        top_old = jnp.full((batch_steps, heads_local, row_count), -1e30, jnp.float32)
        piece_rows = piece.shape[1]
        keys_blk = piece[:, :, 0].reshape(batch_steps, piece_rows, heads_local, HDIM)
        values_blk = piece[:, :, 1].reshape(batch_steps, piece_rows, heads_local, HDIM)
        scores = (
            jnp.einsum("bqhe,bkhe->bhqk", queries, keys_blk, preferred_element_type=jnp.float32)
            * score_scale
        )
        top_new = jnp.maximum(top_old, jnp.max(scores, axis=3))
        weights_exp = jnp.exp(scores - top_new[:, :, :, None])
        total_new = jnp.sum(weights_exp, axis=3)
        update = jnp.einsum(
            "bhqk,bkhe->bqhe",
            weights_exp.astype(jnp.bfloat16),
            values_blk,
            preferred_element_type=jnp.float32,
        )
        accum = update
        top_final, total_final, accum = (top_new, total_new, accum)
        attended = accum / jnp.transpose(total_final, (0, 2, 1))[:, :, :, None]
        attn_mixed = attended.reshape(batch_steps, row_count, heads_local * HDIM).astype(
            jnp.bfloat16
        )
        partial_value = jnp.einsum(
            "brq,dq->brd", attn_mixed, w_proj_all, preferred_element_type=jnp.float32
        )
        head_total = lax.psum(partial_value, "head")
        joined = (hidden + head_total).astype(jnp.bfloat16)
        predicted = jnp.einsum("cd,brd->bcr", w_final, joined, preferred_element_type=jnp.float32)
        drift_term = keep_rate[:, None, None] * states + noise_rate[:, None, None] * predicted
        local_incl = jnp.cumsum(drift_term, axis=0)
        local_total = local_incl[-1]
        earlier = entering(local_total, "step", add_terms, jnp.zeros_like(local_total))
        before = earlier[None] + (local_incl - drift_term)
        new_states = start_noise[None] + before
        change = new_states - states
        square_sum = jnp.sum(change * change)
        summed = lax.psum(square_sum, ("step", "frame"))
        residual_list.append(jnp.sqrt(summed / cell_count + 1e-06))
        states = new_states
    residual_norms = jnp.stack(residual_list)
    trajectory = states + drift_term
    return (trajectory, residual_norms)


def solution(mesh):
    return jax.shard_map(
        local,
        mesh=mesh,
        in_specs=(
            P("parts", "frame"),
            P("frame", None),
            P(),
            P("step"),
            P("step"),
            P(),
            P(),
            P(),
            P(),
            P("step", None, "head"),
            P("step", "head"),
            P(),
        ),
        out_specs=(P("step", "parts", "frame"), P("parts")),
        check_vma=False,
    )
```

profile of v0, /device:TPU:0, one launch (start us, length us, event | category | flops | bytes accessed | tf_op | source)
XLA Modules:
  0.0 354.4 jit_solution(680078700515391486)
XLA Ops:
  7.3 0.7 all-gather.3.cloned.1.call-update
  8.0 0.7 all-gather.5.cloned.1.call-update
  9.6 0.4 multiply_reduce_fusion.3
  10.0 86.9 %all-gather.3.cloned.1.call-done = bf16[1152,3,576]{2,0,1:T(8,128)(2,1)} async-done(((bf16[288,3,576]{2,0,1:T(8,128)(2,1)}), bf16[1152,3,576]{2,0,1:T(8,128)(2,1)}) %all-gather.3.cloned.1.call-update) | async-done | bytes 3981328 | tf_op jit(solution)/shard_map/all_gather | solution.py:43
  96.9 4.0 %fusion.4 = bf16[1,128,3,576]{1,3,2,0:T(8,128)(2,1)S(1)} fusion(bf16[1152,3,576]{2,0,1:T(8,128)(2,1)} %all-gather.3.cloned.1.call-done, f32[128,1152]{1,0:T(8,128)S(1)} %get-tuple-element.432, f32[1152]{0:T(1024)S(1)} %copy-done.6, f32[128]{0:T(128)S(1)} %add_rsqrt_fusion.3), kind=kOutput, calls=%fused_computation.24 | convolution fusion | flops 510271488 | bytes 5018624 | tf_op jit(solution)/shard_map/brd,dkq->brkq/dot_general | solution.py:75
  101.0 9.3 %all_gather.31 = bf16[1,256,2,576]{1,3,2,0:T(8,128)(2,1)S(1)} all-gather(bf16[1,128,2,576]{1,3,2,0:T(8,128)(2,1)S(1)} %slice.64), channel_id=1, replica_groups=mesh['parts'=2,'step'=4,'frame'=2,'head'=2] {'frame'}, dimensions={1}, use_global_device_ids=true | all-gather | bytes 884736 | tf_op jit(solution)/shard_map/all_gather | solution.py:81
  110.3 0.4 fusion.92
  110.8 0.4 fusion.24
  111.2 0.4 fusion.17
  111.6 20.7 %all-gather.5.cloned.1.call-done = bf16[1152,576]{1,0:T(8,128)(2,1)} async-done(((bf16[288,576]{1,0:T(8,128)(2,1)}), bf16[1152,576]{1,0:T(8,128)(2,1)}) %all-gather.5.cloned.1.call-update) | async-done | bytes 1327120 | tf_op jit(solution)/shard_map/all_gather | solution.py:44
  132.3 2.8 convolution_bitcast_fusion.3
  135.8 0.6 fusion.84
  136.5 16.4 %all-reduce.6.cloned.1.call-done = f32[1,128,1152]{2,1,0:T(8,128)} async-done(((f32[1,128,1152]{2,1,0:T(8,128)}), f32[1,128,1152]{2,1,0:T(8,128)}) %all-reduce.6.cloned.1.call-update) | async-done | bytes 589840 | tf_op jit(solution)/shard_map/psum | solution.py:108
  152.9 2.5 fusion.15
  155.4 13.5 %all_gather.33 = f32[4,16,128]{2,1,0:T(8,128)S(1)} all-gather(f32[1,16,128]{2,1,0:T(8,128)S(1)} %fusion.15), channel_id=1, replica_groups=mesh['parts'=2,'step'=4,'frame'=2,'head'=2] {'step'}, dimensions={0}, use_global_device_ids=true | all-gather | bytes 40960 | tf_op jit(solution)/shard_map/all_gather | solution.py:13
  169.4 4.0 %fusion.5 = bf16[1,128,3,576]{1,3,2,0:T(8,128)(2,1)S(1)} fusion(bf16[1152,3,576]{2,0,1:T(8,128)(2,1)} %all-gather.3.cloned.1.call-done, f32[128,1152]{1,0:T(8,128)S(1)} %get-tuple-element.436, f32[128]{0:T(128)S(1)} %add_rsqrt_fusion.2, f32[1152]{0:T(1024)S(1)} %copy-done.6), kind=kOutput, calls=%fused_computation.25 | convolution fusion | flops 510271488 | bytes 5018624 | tf_op jit(solution)/shard_map/brd,dkq->brkq/dot_general | solution.py:75
  173.5 7.4 %all_gather.34 = bf16[1,256,2,576]{1,3,2,0:T(8,128)(2,1)S(1)} all-gather(bf16[1,128,2,576]{1,3,2,0:T(8,128)(2,1)S(1)} %slice.68), channel_id=1, replica_groups=mesh['parts'=2,'step'=4,'frame'=2,'head'=2] {'frame'}, dimensions={1}, use_global_device_ids=true | all-gather | bytes 884736 | tf_op jit(solution)/shard_map/all_gather | solution.py:81
  180.9 0.4 fusion.93
  181.4 0.4 fusion.26
  181.8 0.4 fusion.19
  182.2 0.6 copy-done.1
  182.8 1.4 convolution_bitcast_fusion.2
  184.3 19.7 %all-reduce.8.cloned.1.call-done = f32[1,128,1152]{2,1,0:T(8,128)} async-done(((f32[1,128,1152]{2,1,0:T(8,128)}), f32[1,128,1152]{2,1,0:T(8,128)}) %all-reduce.8.cloned.1.call-update) | async-done | bytes 589840 | tf_op jit(solution)/shard_map/psum | solution.py:108
  203.9 2.5 fusion.13
  206.4 13.5 %all_gather.35 = f32[4,16,128]{2,1,0:T(8,128)S(1)} all-gather(f32[1,16,128]{2,1,0:T(8,128)S(1)} %fusion.13), channel_id=1, replica_groups=mesh['parts'=2,'step'=4,'frame'=2,'head'=2] {'step'}, dimensions={0}, use_global_device_ids=true | all-gather | bytes 40960 | tf_op jit(solution)/shard_map/all_gather | solution.py:13
  220.1 0.4 multiply_reduce_fusion.1
  220.4 4.0 %fusion.6 = bf16[1,128,3,576]{1,3,2,0:T(8,128)(2,1)S(1)} fusion(bf16[1152,3,576]{2,0,1:T(8,128)(2,1)} %all-gather.3.cloned.1.call-done, f32[128,1152]{1,0:T(8,128)S(1)} %get-tuple-element.440, f32[128]{0:T(128)S(1)} %add_rsqrt_fusion.1, f32[1152]{0:T(1024)S(1)} %copy-done.6), kind=kOutput, calls=%fused_computation.26 | convolution fusion | flops 510271488 | bytes 5018624 | tf_op jit(solution)/shard_map/brd,dkq->brkq/dot_general | solution.py:75
  224.5 7.4 %all_gather.36 = bf16[1,256,2,576]{1,3,2,0:T(8,128)(2,1)S(1)} all-gather(bf16[1,128,2,576]{1,3,2,0:T(8,128)(2,1)S(1)} %slice.72), channel_id=1, replica_groups=mesh['parts'=2,'step'=4,'frame'=2,'head'=2] {'frame'}, dimensions={1}, use_global_device_ids=true | all-gather | bytes 884736 | tf_op jit(solution)/shard_map/all_gather | solution.py:81
  232.0 0.4 fusion.94
  232.4 0.4 fusion.28
  232.8 0.4 fusion.21
  233.2 1.4 convolution_bitcast_fusion.1
  234.9 19.5 %all-reduce.10.cloned.1.call-done = f32[1,128,1152]{2,1,0:T(8,128)} async-done(((f32[1,128,1152]{2,1,0:T(8,128)}), f32[1,128,1152]{2,1,0:T(8,128)}) %all-reduce.10.cloned.1.call-update) | async-done | bytes 589840 | tf_op jit(solution)/shard_map/psum | solution.py:108
  254.4 2.5 fusion.11
  256.9 13.5 %all_gather.37 = f32[4,16,128]{2,1,0:T(8,128)S(1)} all-gather(f32[1,16,128]{2,1,0:T(8,128)S(1)} %fusion.11), channel_id=1, replica_groups=mesh['parts'=2,'step'=4,'frame'=2,'head'=2] {'step'}, dimensions={0}, use_global_device_ids=true | all-gather | bytes 40960 | tf_op jit(solution)/shard_map/all_gather | solution.py:13
  270.5 0.4 multiply_reduce_fusion
  270.9 4.0 %fusion.7 = bf16[1,128,3,576]{1,3,2,0:T(8,128)(2,1)S(1)} fusion(bf16[1152,3,576]{2,0,1:T(8,128)(2,1)} %all-gather.3.cloned.1.call-done, f32[128,1152]{1,0:T(8,128)S(1)} %get-tuple-element.444, f32[128]{0:T(128)S(1)} %add_rsqrt_fusion, f32[1152]{0:T(1024)S(1)} %copy-done.6), kind=kOutput, calls=%fused_computation.27 | convolution fusion | flops 510271488 | bytes 5018624 | tf_op jit(solution)/shard_map/brd,dkq->brkq/dot_general | solution.py:75
  275.0 7.4 %all_gather.38 = bf16[1,256,2,576]{1,3,2,0:T(8,128)(2,1)S(1)} all-gather(bf16[1,128,2,576]{1,3,2,0:T(8,128)(2,1)S(1)} %slice.76), channel_id=1, replica_groups=mesh['parts'=2,'step'=4,'frame'=2,'head'=2] {'frame'}, dimensions={1}, use_global_device_ids=true | all-gather | bytes 884736 | tf_op jit(solution)/shard_map/all_gather | solution.py:81
  282.5 0.4 fusion.95
  282.9 0.4 fusion.30
  283.3 0.4 fusion.23
  283.7 1.4 convolution_bitcast_fusion
  285.1 19.7 %all-reduce.12.cloned.1.call-done = f32[1,128,1152]{2,1,0:T(8,128)} async-done(((f32[1,128,1152]{2,1,0:T(8,128)}), f32[1,128,1152]{2,1,0:T(8,128)}) %all-reduce.12.cloned.1.call-update) | async-done | bytes 589840 | tf_op jit(solution)/shard_map/psum | solution.py:108
  304.9 2.5 fusion.9
  307.3 13.5 %all_gather.39 = f32[4,16,128]{2,1,0:T(8,128)S(1)} all-gather(f32[1,16,128]{2,1,0:T(8,128)S(1)} %fusion.9), channel_id=1, replica_groups=mesh['parts'=2,'step'=4,'frame'=2,'head'=2] {'step'}, dimensions={0}, use_global_device_ids=true | all-gather | bytes 40960 | tf_op jit(solution)/shard_map/all_gather | solution.py:13
  321.0 1.3 fusion.73
  322.2 22.0 %all-reduce = (f32[]{:T(128)}, f32[]{:T(128)}, f32[]{:T(128)}, f32[]{:T(128)}) all-reduce(f32[]{:T(128)} %get-tuple-element.383, f32[]{:T(128)} %get-tuple-element.384, f32[]{:T(128)} %get-tuple-element.385, f32[]{:T(128)} %get-tuple-element.382), channel_id=1, replica_groups=mesh['parts'=2,'step'=4,'frame'=2,'head'=2] {'step','frame'}, use_global_device_ids=true, to_apply=%region_33.34 | all-reduce | flops 4 | bytes 32 | tf_op jit(solution)/shard_map/psum | solution.py:119
  347.0 0.6 pad_maximum_fusion
  (76 shorter events, 1.9 us)
Async XLA Ops:
  7.2 2.2 copy-start
  7.2 2.4 copy-start.5
  7.2 2.4 copy-start.2
  7.2 2.4 copy-start.3
  7.2 89.7 %copy-start.6 = (f32[1152]{0:T(1024)S(1)}, f32[1152]{0:T(1024)}, u32[]{:S(2)}) copy-start(f32[1152]{0:T(1024)} %param.28) | copy-start | bytes 13828
  7.2 89.7 %all-gather.3.cloned.1.call-start = ((), (), s32[]{:S(2)}) async-start(), calls=%async_computation | async-start | bytes 5529600 | tf_op jit(solution)/shard_map/all_gather | solution.py:43
  8.0 124.3 %all-gather.5.cloned.1.call-start = ((), (), s32[]{:S(2)}) async-start(), calls=%async_computation.1 | async-start | bytes 1843200 | tf_op jit(solution)/shard_map/all_gather | solution.py:44
  8.7 144.2 %all-reduce.6.cloned.1.call-start = ((), (), s32[]{:S(2)}) async-start(), calls=%async_computation.2 | async-start | bytes 1179648 | tf_op jit(solution)/shard_map/psum | solution.py:108
  111.6 24.2 %copy-start.7 = (f32[128]{0:T(128)S(1)}, f32[128]{0:T(128)}, u32[]{:S(2)}) copy-start(f32[128]{0:T(128)} %param.25) | copy-start | bytes 1540
  111.6 24.2 %copy-start.8 = (f32[128]{0:T(128)S(1)}, f32[128]{0:T(128)}, u32[]{:S(2)}) copy-start(f32[128]{0:T(128)} %param.26) | copy-start | bytes 1540
  111.6 41.3 %copy-start.4 = (bf16[16,1152]{1,0:T(8,128)(2,1)S(1)}, bf16[16,1152]{1,0:T(8,128)(2,1)}, u32[]{:S(2)}) copy-start(bf16[16,1152]{1,0:T(8,128)(2,1)} %param.31) | copy-start | bytes 110596
  135.1 68.9 %all-reduce.8.cloned.1.call-start = ((), (), s32[]{:S(2)}) async-start(), calls=%async_computation.3 | async-start | bytes 1179648 | tf_op jit(solution)/shard_map/psum | solution.py:108
  181.4 1.4 copy-start.1
  184.2 70.2 %all-reduce.10.cloned.1.call-start = ((), (), s32[]{:S(2)}) async-start(), calls=%async_computation.4 | async-start | bytes 1179648 | tf_op jit(solution)/shard_map/psum | solution.py:108
  234.7 70.2 %all-reduce.12.cloned.1.call-start = ((), (), s32[]{:S(2)}) async-start(), calls=%async_computation.5 | async-start | bytes 1179648 | tf_op jit(solution)/shard_map/psum | solution.py:108
Sparse Core Ops, SparseCore 0:
  9.6 87.2 all-gather.2
  98.4 33.7 all-gather.4
  135.2 17.6 all-reduce.5
  184.3 19.5 all-reduce.7
  234.8 19.5 all-reduce.9
  285.2 19.5 all-reduce.11
where the time goes:
time: 355 us; the launch traced here: 354 us
  waiting for transfers between devices  184 us (52%)
  blocking collectives  108 us (30%)
  matrix products  38 us (11%)
  between operations  18.5 us (5%)
  other arithmetic  4.24 us (1%)
    all_gather x1, waiting for transfers between devices, local(): lax.all_gather(w_qkv, 'step', axis=0, tiled=True)  86.9 us
    psum x4, waiting for transfers between devices, local(): head_total = lax.psum(partial_value, 'head')  75.4 us
    all_gather x4, blocking collectives, entering(): everything = lax.all_gather(value, axis)  54.1 us
    all_gather x4, blocking collectives, local(): piece = lax.all_gather(keys_values, 'frame', axis=1, tiled=True)  31.6 us
    psum x1, blocking collectives, local(): summed = lax.psum(square_sum, ('step', 'frame'))  22 us
    all_gather x1, waiting for transfers between devices, local(): lax.all_gather(w_proj, 'step', axis=0, tiled=True)  20.7 us
    dot_general x4, matrix products, local(): jnp.einsum('brd,dkq->brkq', normed, w_qkv_all, preferred_element_type=jnp...  16.1 us
    dot_general x4, matrix products, local(): jnp.einsum('cd,brd->bcr', w_final, joined, preferred_element_type=jnp.flo...  9.96 us
  transfers between devices with their start and end apart: 6, of which 6 were waited for; matrix products, arithmetic and copies ran while one was open for 2% of the time, Pallas kernels for 0%

commit v1 on v0

--- a/solution.py
+++ b/solution.py
@@ -105,7 +105,8 @@
         partial_value = jnp.einsum(
             "brq,dq->brd", attn_mixed, w_proj_all, preferred_element_type=jnp.float32
         )
-        head_total = lax.psum(partial_value, "head")
+        blocks = lax.all_gather(partial_value, "head", axis=0, tiled=False)
+        head_total = blocks.sum(axis=0)
         joined = (hidden + head_total).astype(jnp.bfloat16)
         predicted = jnp.einsum("cd,brd->bcr", w_final, joined, preferred_element_type=jnp.float32)
         drift_term = keep_rate[:, None, None] * states + noise_rate[:, None, None] * predicted

time: 355 us -> 319 us (0.90)
  waiting for transfers between devices: 184 us -> 146 us
  other arithmetic: 4.24 us -> 10.5 us
  matrix products: 38 us -> 33.7 us
    psum x4 -> x0, waiting for transfers between devices: 75.4 us -> none  [local(): head_total = lax.psum(partial_value, 'head')]
    all_gather x0 -> x4, waiting for transfers between devices: none -> 37 us  [local(): blocks = lax.all_gather(partial_value, 'head', axis=0, tiled=False)]
    reduce_sum x0 -> x5, other arithmetic: none -> 6.26 us  [the longest x4 5.61 us: local(): head_total = blocks.sum(axis=0)]
    dot_general x4, matrix products: 9.96 us -> 5.67 us  [local(): jnp.einsum('cd,brd->bcr', w_final, joined, preferred_element_type=jnp.flo...]
where the time goes in v1:
time: 319 us; the launch traced here: 318 us
  waiting for transfers between devices  146 us (46%)
  blocking collectives  108 us (34%)
  matrix products  33.7 us (11%)
  between operations  18.5 us (6%)
  other arithmetic  10.5 us (3%)
    all_gather x1, waiting for transfers between devices, local(): lax.all_gather(w_qkv, 'step', axis=0, tiled=True)  86.9 us
    all_gather x4, blocking collectives, entering(): everything = lax.all_gather(value, axis)  53.9 us
    all_gather x4, waiting for transfers between devices, local(): blocks = lax.all_gather(partial_value, 'head', axis=0, tiled=False)  37 us
    all_gather x4, blocking collectives, local(): piece = lax.all_gather(keys_values, 'frame', axis=1, tiled=True)  31.8 us
    psum x1, blocking collectives, local(): summed = lax.psum(square_sum, ('step', 'frame'))  22 us
    all_gather x1, waiting for transfers between devices, local(): lax.all_gather(w_proj, 'step', axis=0, tiled=True)  20.7 us
    dot_general x4, matrix products, local(): jnp.einsum('brd,dkq->brkq', normed, w_qkv_all, preferred_element_type=jnp...  16.1 us
    dot_general x4, matrix products, local(): jnp.einsum('brq,dq->brd', attn_mixed, w_proj_all, preferred_element_type=...  7.05 us
  transfers between devices with their start and end apart: 6, of which 6 were waited for; matrix products, arithmetic and copies ran while one was open for 2% of the time, Pallas kernels for 0%

profile of v1, /device:TPU:0, one launch (start us, length us, event | category | flops | bytes accessed | tf_op | source)
XLA Modules:
  0.0 317.9 jit_solution(2549496247262070554)
XLA Ops:
  7.3 0.7 all-gather.11.cloned.1.call-update
  8.0 0.7 all-gather.13.cloned.1.call-update
  10.0 86.9 %all-gather.11.cloned.1.call-done = bf16[1152,3,576]{2,0,1:T(8,128)(2,1)} async-done(((bf16[288,3,576]{2,0,1:T(8,128)(2,1)}), bf16[1152,3,576]{2,0,1:T(8,128)(2,1)}) %all-gather.11.cloned.1.call-update) | async-done | bytes 3981328 | tf_op jit(solution)/shard_map/all_gather | solution.py:43
  96.9 4.0 %fusion.4 = bf16[1,128,3,576]{1,3,2,0:T(8,128)(2,1)S(1)} fusion(bf16[1152,3,576]{2,0,1:T(8,128)(2,1)} %all-gather.11.cloned.1.call-done, f32[128,1152]{1,0:T(8,128)S(1)} %get-tuple-element.432, f32[1152]{0:T(1024)S(1)} %copy-done.6, f32[128]{0:T(128)S(1)} %add_rsqrt_fusion.3), kind=kOutput, calls=%fused_computation.20 | convolution fusion | flops 510271488 | bytes 5018624 | tf_op jit(solution)/shard_map/brd,dkq->brkq/dot_general | solution.py:75
  100.9 9.3 %all_gather.55 = bf16[1,256,2,576]{1,3,2,0:T(8,128)(2,1)S(1)} all-gather(bf16[1,128,2,576]{1,3,2,0:T(8,128)(2,1)S(1)} %slice.64), channel_id=1, replica_groups=mesh['parts'=2,'step'=4,'frame'=2,'head'=2] {'frame'}, dimensions={1}, use_global_device_ids=true | all-gather | bytes 884736 | tf_op jit(solution)/shard_map/all_gather | solution.py:81
  110.3 0.4 fusion.80
  110.8 0.4 fusion.24
  111.1 0.4 fusion.17
  111.6 20.7 %all-gather.13.cloned.1.call-done = bf16[1152,576]{1,0:T(8,128)(2,1)} async-done(((bf16[288,576]{1,0:T(8,128)(2,1)}), bf16[1152,576]{1,0:T(8,128)(2,1)}) %all-gather.13.cloned.1.call-update) | async-done | bytes 1327120 | tf_op jit(solution)/shard_map/all_gather | solution.py:44
  132.3 2.8 fusion.84
  135.8 0.6 fusion.72
  136.4 0.7 fusion.73
  137.1 6.3 %all-gather.15.cloned.1.call-done = f32[256,1152]{1,0:T(8,128)} async-done(((f32[128,1152]{1,0:T(8,128)}), f32[256,1152]{1,0:T(8,128)}) %all-gather.15.cloned.1.call-update) | async-done | bytes 1179664 | tf_op jit(solution)/shard_map/all_gather | solution.py:108
  143.4 1.4 reduce.32
  144.8 1.4 fusion.15
  146.2 13.5 %all_gather.59 = f32[4,16,128]{2,1,0:T(8,128)S(1)} all-gather(f32[1,16,128]{2,1,0:T(8,128)S(1)} %fusion.15), channel_id=1, replica_groups=mesh['parts'=2,'step'=4,'frame'=2,'head'=2] {'step'}, dimensions={0}, use_global_device_ids=true | all-gather | bytes 40960 | tf_op jit(solution)/shard_map/all_gather | solution.py:13
  160.2 4.0 %fusion.5 = bf16[1,128,3,576]{1,3,2,0:T(8,128)(2,1)S(1)} fusion(bf16[1152,3,576]{2,0,1:T(8,128)(2,1)} %all-gather.11.cloned.1.call-done, f32[128,1152]{1,0:T(8,128)S(1)} %get-tuple-element.436, f32[128]{0:T(128)S(1)} %add_rsqrt_fusion.2, f32[1152]{0:T(1024)S(1)} %copy-done.6), kind=kOutput, calls=%fused_computation.21 | convolution fusion | flops 510271488 | bytes 5018624 | tf_op jit(solution)/shard_map/brd,dkq->brkq/dot_general | solution.py:75
  164.3 7.4 %all_gather.60 = bf16[1,256,2,576]{1,3,2,0:T(8,128)(2,1)S(1)} all-gather(bf16[1,128,2,576]{1,3,2,0:T(8,128)(2,1)S(1)} %slice.68), channel_id=1, replica_groups=mesh['parts'=2,'step'=4,'frame'=2,'head'=2] {'frame'}, dimensions={1}, use_global_device_ids=true | all-gather | bytes 884736 | tf_op jit(solution)/shard_map/all_gather | solution.py:81
  171.7 0.4 fusion.81
  172.6 0.4 fusion.19
  173.0 0.6 copy-done.1
  173.5 1.4 fusion.85
  175.0 10.2 %all-gather.17.cloned.1.call-done = f32[256,1152]{1,0:T(8,128)} async-done(((f32[128,1152]{1,0:T(8,128)}), f32[256,1152]{1,0:T(8,128)}) %all-gather.17.cloned.1.call-update) | async-done | bytes 1179664 | tf_op jit(solution)/shard_map/all_gather | solution.py:108
  185.3 1.4 reduce.33
  186.7 1.4 fusion.13
  188.1 13.5 %all_gather.63 = f32[4,16,128]{2,1,0:T(8,128)S(1)} all-gather(f32[1,16,128]{2,1,0:T(8,128)S(1)} %fusion.13), channel_id=1, replica_groups=mesh['parts'=2,'step'=4,'frame'=2,'head'=2] {'step'}, dimensions={0}, use_global_device_ids=true | all-gather | bytes 40960 | tf_op jit(solution)/shard_map/all_gather | solution.py:13
  202.1 4.0 %fusion.6 = bf16[1,128,3,576]{1,3,2,0:T(8,128)(2,1)S(1)} fusion(bf16[1152,3,576]{2,0,1:T(8,128)(2,1)} %all-gather.11.cloned.1.call-done, f32[128,1152]{1,0:T(8,128)S(1)} %get-tuple-element.440, f32[128]{0:T(128)S(1)} %add_rsqrt_fusion.1, f32[1152]{0:T(1024)S(1)} %copy-done.6), kind=kOutput, calls=%fused_computation.22 | convolution fusion | flops 510271488 | bytes 5018624 | tf_op jit(solution)/shard_map/brd,dkq->brkq/dot_general | solution.py:75
  206.1 7.6 %all_gather.64 = bf16[1,256,2,576]{1,3,2,0:T(8,128)(2,1)S(1)} all-gather(bf16[1,128,2,576]{1,3,2,0:T(8,128)(2,1)S(1)} %slice.72), channel_id=1, replica_groups=mesh['parts'=2,'step'=4,'frame'=2,'head'=2] {'frame'}, dimensions={1}, use_global_device_ids=true | all-gather | bytes 884736 | tf_op jit(solution)/shard_map/all_gather | solution.py:81
  213.8 0.4 fusion.82
  214.6 0.4 fusion.21
  215.0 1.4 fusion.86
  216.5 10.2 %all-gather.19.cloned.1.call-done = f32[256,1152]{1,0:T(8,128)} async-done(((f32[128,1152]{1,0:T(8,128)}), f32[256,1152]{1,0:T(8,128)}) %all-gather.19.cloned.1.call-update) | async-done | bytes 1179664 | tf_op jit(solution)/shard_map/all_gather | solution.py:108
  226.7 1.4 reduce.34
  228.1 1.4 fusion.11
  229.5 13.5 %all_gather.67 = f32[4,16,128]{2,1,0:T(8,128)S(1)} all-gather(f32[1,16,128]{2,1,0:T(8,128)S(1)} %fusion.11), channel_id=1, replica_groups=mesh['parts'=2,'step'=4,'frame'=2,'head'=2] {'step'}, dimensions={0}, use_global_device_ids=true | all-gather | bytes 40960 | tf_op jit(solution)/shard_map/all_gather | solution.py:13
  243.5 4.0 %fusion.7 = bf16[1,128,3,576]{1,3,2,0:T(8,128)(2,1)S(1)} fusion(bf16[1152,3,576]{2,0,1:T(8,128)(2,1)} %all-gather.11.cloned.1.call-done, f32[128,1152]{1,0:T(8,128)S(1)} %get-tuple-element.444, f32[128]{0:T(128)S(1)} %add_rsqrt_fusion, f32[1152]{0:T(1024)S(1)} %copy-done.6), kind=kOutput, calls=%fused_computation.23 | convolution fusion | flops 510271488 | bytes 5018624 | tf_op jit(solution)/shard_map/brd,dkq->brkq/dot_general | solution.py:75
  247.6 7.4 %all_gather.68 = bf16[1,256,2,576]{1,3,2,0:T(8,128)(2,1)S(1)} all-gather(bf16[1,128,2,576]{1,3,2,0:T(8,128)(2,1)S(1)} %slice.76), channel_id=1, replica_groups=mesh['parts'=2,'step'=4,'frame'=2,'head'=2] {'frame'}, dimensions={1}, use_global_device_ids=true | all-gather | bytes 884736 | tf_op jit(solution)/shard_map/all_gather | solution.py:81
  255.0 0.4 fusion.83
  255.5 0.4 fusion.30
  255.9 0.4 fusion.23
  256.3 1.4 fusion.87
  257.7 10.3 %all-gather.21.cloned.1.call-done = f32[256,1152]{1,0:T(8,128)} async-done(((f32[128,1152]{1,0:T(8,128)}), f32[256,1152]{1,0:T(8,128)}) %all-gather.21.cloned.1.call-update) | async-done | bytes 1179664 | tf_op jit(solution)/shard_map/all_gather | solution.py:108
  268.0 1.4 reduce.35
  269.4 1.4 fusion.9
  270.8 13.5 %all_gather.71 = f32[4,16,128]{2,1,0:T(8,128)S(1)} all-gather(f32[1,16,128]{2,1,0:T(8,128)S(1)} %fusion.9), channel_id=1, replica_groups=mesh['parts'=2,'step'=4,'frame'=2,'head'=2] {'step'}, dimensions={0}, use_global_device_ids=true | all-gather | bytes 40960 | tf_op jit(solution)/shard_map/all_gather | solution.py:13
  284.4 1.3 fusion.61
  285.7 22.0 %all-reduce = (f32[]{:T(128)}, f32[]{:T(128)}, f32[]{:T(128)}, f32[]{:T(128)}) all-reduce(f32[]{:T(128)} %get-tuple-element.383, f32[]{:T(128)} %get-tuple-element.384, f32[]{:T(128)} %get-tuple-element.385, f32[]{:T(128)} %get-tuple-element.382), channel_id=1, replica_groups=mesh['parts'=2,'step'=4,'frame'=2,'head'=2] {'step','frame'}, use_global_device_ids=true, to_apply=%region_33.34 | all-reduce | flops 4 | bytes 32 | tf_op jit(solution)/shard_map/psum | solution.py:120
  310.4 0.6 pad_maximum_fusion
  (81 shorter events, 3.6 us)
Async XLA Ops:
  7.2 2.2 copy-start
  7.2 2.4 copy-start.5
  7.2 2.4 copy-start.2
  7.2 2.4 copy-start.3
  7.2 89.7 %copy-start.6 = (f32[1152]{0:T(1024)S(1)}, f32[1152]{0:T(1024)}, u32[]{:S(2)}) copy-start(f32[1152]{0:T(1024)} %param.28) | copy-start | bytes 13828
  7.2 89.7 %all-gather.11.cloned.1.call-start = ((), (), s32[]{:S(2)}) async-start(), calls=%async_computation | async-start | bytes 5529600 | tf_op jit(solution)/shard_map/all_gather | solution.py:43
  8.0 124.3 %all-gather.13.cloned.1.call-start = ((), (), s32[]{:S(2)}) async-start(), calls=%async_computation.1 | async-start | bytes 1843200 | tf_op jit(solution)/shard_map/all_gather | solution.py:44
  8.7 134.7 %all-gather.15.cloned.1.call-start = ((), (), s32[]{:S(2)}) async-start(), calls=%async_computation.2 | async-start | bytes 1769472 | tf_op jit(solution)/shard_map/all_gather | solution.py:108
  111.5 24.2 %copy-start.7 = (f32[128]{0:T(128)S(1)}, f32[128]{0:T(128)}, u32[]{:S(2)}) copy-start(f32[128]{0:T(128)} %param.25) | copy-start | bytes 1540
  111.5 24.9 %copy-start.8 = (f32[128]{0:T(128)S(1)}, f32[128]{0:T(128)}, u32[]{:S(2)}) copy-start(f32[128]{0:T(128)} %param.26) | copy-start | bytes 1540
  135.0 9.8 %copy-start.4 = (bf16[16,1152]{1,0:T(8,128)(2,1)S(1)}, bf16[16,1152]{1,0:T(8,128)(2,1)}, u32[]{:S(2)}) copy-start(bf16[16,1152]{1,0:T(8,128)(2,1)} %param.31) | copy-start | bytes 110596
  135.1 50.2 %all-gather.17.cloned.1.call-start = ((), (), s32[]{:S(2)}) async-start(), calls=%async_computation.3 | async-start | bytes 1769472 | tf_op jit(solution)/shard_map/all_gather | solution.py:108
  172.2 1.4 copy-start.1
  175.0 51.7 %all-gather.19.cloned.1.call-start = ((), (), s32[]{:S(2)}) async-start(), calls=%async_computation.4 | async-start | bytes 1769472 | tf_op jit(solution)/shard_map/all_gather | solution.py:108
  216.4 51.6 %all-gather.21.cloned.1.call-start = ((), (), s32[]{:S(2)}) async-start(), calls=%async_computation.5 | async-start | bytes 1769472 | tf_op jit(solution)/shard_map/all_gather | solution.py:108
Sparse Core Ops, SparseCore 0:
  9.6 87.2 all-gather.10
  98.4 33.7 all-gather.12
  135.2 8.1 all-gather.14
  175.1 10.1 all-gather.16
  216.6 10.0 all-gather.18
  257.9 10.0 all-gather.20
